TPU v7x, 32 devices: a whole 2x2x4 slice. The times are simulated.
32 devices in a mesh: group: 4 (over x, core), shard: 8 (over z, y).
Axes of the slice: x: 2, y: 2, z: 4, core: 2. Of those that a mesh axis runs over, the one named last changes fastest.
Arguments:
- hidden: bfloat16 [8192, 768], P(('group', 'shard')), may hold values from -40 to 40
- out_grads: bfloat16 [5, 8192, 768], P(None, ('group', 'shard')), may hold values from -40 to 40
- global_inputs: bfloat16 [1024, 768], P(('group', 'shard')), may hold values from -40 to 40
- query_grads: bfloat16 [1024, 768], P(('group', 'shard')), may hold values from -40 to 40
- weight_grads: bfloat16 [6, 768, 768], P(None, 'shard'), may hold values from -48 to 48
- momentum: float32 [6, 768, 768], P(None, 'shard', 'group'), may hold values from -6 to 6
Outputs:
- new_momentum: float32 [6, 768, 768], P(None, 'shard', 'group')
All inputs are finite; a program needn't handle non-finite values. Where the computation divides by a largest or mean magnitude, that divisor is 1e-20 or more.
Results may differ from a plain program's by a relative error of at most 0.0018.
Values may be sent and summed in bfloat16 or wider, within the bound.
A program may use at most 128 MiB of HBM per device.

v0:
```python
import jax
import jax.numpy as jnp
from jax import lax
from jax.sharding import PartitionSpec as P

ITERS = 3
PRECISE = lax.Precision.HIGHEST
DAMPING = 0.1
MOMENTUM = 0.9


def broadcast(array, axis, root):
    mine = lax.axis_index(axis) == root
    return lax.psum(jnp.where(mine, array, jnp.zeros_like(array)), axis)


def outer_sum(matrix_rows):
    return lax.dot_general(
        matrix_rows, matrix_rows, (((0,), (0,)), ((), ())), preferred_element_type=jnp.float32
    )


def on_device(hidden, out_grads, global_inputs, query_grads, weight_grads, momentum):
    model_width = hidden.shape[1]
    group_size = lax.axis_size("group")
    shard_size = lax.axis_size("shard")
    per_group = 8 // group_size
    row_block = model_width // shard_size
    col_block = momentum.shape[2]
    shard_pos = lax.axis_index("shard")
    group_pos = lax.axis_index("group")
    devices = group_size * shard_size
    partials = [outer_sum(hidden), outer_sum(global_inputs)]
    partials = partials + [outer_sum(out_grads[member]) for member in range(5)]
    partials = partials + [outer_sum(query_grads)]
    stacked = jnp.stack([single.astype(jnp.bfloat16) for single in partials])
    summed = lax.psum_scatter(stacked, "group", scatter_dimension=0, tiled=True).astype(jnp.float32)
    factor_ids = group_pos * per_group + jnp.arange(per_group)
    is_global = (factor_ids == 1) | (factor_ids == 7)
    samp_total = float(hidden.shape[0] * devices)
    glob_total = float(global_inputs.shape[0] * devices)
    counted = jnp.where(is_global, glob_total, samp_total).astype(jnp.float32)
    factor_full = lax.psum(summed, "shard")
    covariance = factor_full / counted[:, None, None]
    mean_diag = jnp.trace(covariance, axis1=1, axis2=2) / model_width
    eye_full = jnp.eye(model_width, dtype=jnp.float32)
    matrix = covariance / mean_diag[:, None, None] + DAMPING * eye_full
    row_limit = jnp.max(jnp.sum(jnp.abs(matrix), axis=2), axis=1)
    approx = jnp.broadcast_to(eye_full, matrix.shape) / row_limit[:, None, None]
    for iteration in range(ITERS):
        product = jnp.einsum("kij,kjl->kil", matrix, approx, precision=PRECISE)
        approx = 2.0 * approx - jnp.einsum("kij,kjl->kil", approx, product, precision=PRECISE)
    own_rows = lax.dynamic_slice_in_dim(approx, shard_pos * row_block, row_block, 1)
    all_rows = lax.all_gather(own_rows, "group", axis=0, tiled=True)
    input_inv = jnp.stack(
        [broadcast(approx[factor % per_group], "group", factor // per_group) for factor in range(2)]
    )
    input_cols = lax.dynamic_slice_in_dim(input_inv, group_pos * col_block, col_block, 2)
    out_inverse = all_rows[2:8]
    initial = jnp.zeros(out_inverse.shape, jnp.float32)
    gathered = lax.all_gather(weight_grads, "shard", axis=1, tiled=True)
    columns = lax.slice_in_dim(out_inverse, 0, gathered.shape[1], axis=2)
    left_side = initial + jnp.einsum(
        "wrn,wnd->wrd", columns, gathered.astype(jnp.float32), precision=PRECISE
    )
    local_part = jnp.einsum("wrd,de->wre", left_side[0:5], input_cols[0], precision=PRECISE)
    global_part = jnp.dot(left_side[5], input_cols[1], precision=PRECISE)[None]
    return MOMENTUM * momentum + jnp.concatenate([local_part, global_part], axis=0)


def solution(mesh):
    placed = (
        P(("group", "shard"), None),
        P(None, ("group", "shard"), None),
        P(("group", "shard"), None),
        P(("group", "shard"), None),
        P(None, "shard", None),
        P(None, "shard", "group"),
    )
    return jax.shard_map(
        on_device, mesh=mesh, in_specs=placed, out_specs=P(None, "shard", "group"), check_vma=False
    )
```

profile of v0, /device:TPU:0, one launch (start us, length us, event | category | flops | bytes accessed | tf_op | source)
XLA Modules:
  0.0 529.7 jit_solution(5312361933273675997)
XLA Ops:
  9.9 2.4 fusion.10
  12.3 2.7 fusion.16
  15.0 1.6 fusion.18
  16.6 1.6 fusion.20
  18.1 1.6 fusion.22
  21.2 1.6 fusion.12
  23.3 1.5 fusion.26
  24.8 79.3 %reduce-scatter.2.cloned.1.call-done = bf16[2,768,768]{2,1,0:T(8,128)(2,1)} async-done(((bf16[8,768,768]{2,1,0:T(8,128)(2,1)}), bf16[2,768,768]{2,1,0:T(8,128)(2,1)}) %reduce-scatter.2.cloned.1.call-update) | async-done | bytes 2359312 | tf_op jit(solution)/shard_map/reduce_scatter | solution.py:37
  104.1 187.7 %all-reduce.5 = f32[2,768,768]{2,1,0:T(8,128)} all-reduce(bf16[2,768,768]{2,1,0:T(8,128)(2,1)} %reduce-scatter.2.cloned.1.call-done), channel_id=1, replica_groups=mesh['group'=4,'shard'=8] {'shard'}, use_global_device_ids=true, to_apply=%region_1.2 | all-reduce | flops 1179648 | bytes 7077888 | tf_op jit(solution)/shard_map/psum | solution.py:43
  291.9 3.7 select_reduce_fusion
  295.6 3.0 abs_reduce_fusion
  298.7 15.6 %fusion.2 = f32[2,768,768]{2,1,0:T(8,128)S(1)} fusion(f32[2,768,768]{2,1,0:T(8,128)} %get-tuple-element.8, f32[2]{0:T(128)S(1)} %reduce_max.9, f32[768,768]{1,0:T(8,128)} %fusion.26), kind=kOutput, calls=%fused_computation.10 | convolution fusion | flops 10872815616 | bytes 11796488 | tf_op jit(solution)/shard_map/kij,kjl->kil/dot_general | solution.py:51
  314.3 12.8 %multiply_subtract_fusion.2 = f32[2,768,768]{2,1,0:T(8,128)S(1)} fusion(f32[2]{0:T(128)S(1)} %reduce_max.9, f32[768,768]{1,0:T(8,128)S(1)} %copy-done.4, f32[2,768,768]{2,1,0:T(8,128)S(1)} %fusion.2), kind=kOutput, calls=%fused_computation.4 | convolution fusion | flops 10876354560 | bytes 11796488 | tf_op jit(solution)/shard_map/kij,kjl->kil/dot_general | solution.py:52
  327.2 12.1 %fusion.40 = f32[2,768,768]{2,1,0:T(8,128)S(1)} fusion(f32[2,768,768]{2,1,0:T(8,128)S(1)} %bitcast.80, f32[2,768,768]{2,1,0:T(8,128)S(1)} %multiply_subtract_fusion.2), kind=kOutput, calls=%fused_computation.65 | convolution fusion | flops 10871635968 | bytes 14155776 | tf_op jit(solution)/shard_map/kij,kjl->kil/dot_general | solution.py:51
  339.3 12.7 %multiply_subtract_fusion.1 = f32[2,768,768]{2,1,0:T(8,128)S(1)} fusion(f32[2,768,768]{2,1,0:T(8,128)S(1)} %multiply_subtract_fusion.2, f32[2,768,768]{2,1,0:T(8,128)S(1)} %fusion.40), kind=kOutput, calls=%fused_computation.3 | convolution fusion | flops 10873995264 | bytes 14155776 | tf_op jit(solution)/shard_map/kij,kjl->kil/dot_general | solution.py:52
  352.0 12.3 %fusion.41 = f32[2,768,768]{2,1,0:T(8,128)S(1)} fusion(f32[2,768,768]{2,1,0:T(8,128)S(1)} %bitcast.80, f32[2,768,768]{2,1,0:T(8,128)S(1)} %multiply_subtract_fusion.1), kind=kOutput, calls=%fused_computation.66 | convolution fusion | flops 10871635968 | bytes 14155776 | tf_op jit(solution)/shard_map/kij,kjl->kil/dot_general | solution.py:51
  364.3 12.5 %multiply_subtract_fusion = f32[2,768,768]{2,1,0:T(8,128)S(1)} fusion(f32[2,768,768]{2,1,0:T(8,128)S(1)} %multiply_subtract_fusion.1, f32[2,768,768]{2,1,0:T(8,128)S(1)} %fusion.41), kind=kOutput, calls=%fused_computation.2 | convolution fusion | flops 10873995264 | bytes 14155776 | tf_op jit(solution)/shard_map/kij,kjl->kil/dot_general | solution.py:52
  376.8 2.6 slice_select_fusion
  381.1 1.9 constant_dynamic-slice_fusion
  383.1 89.3 %all-reduce.4.cloned.1.call-done = (f32[1,768,768]{2,1,0:T(8,128)}, f32[1,768,768]{2,1,0:T(8,128)}) async-done(((f32[1,768,768]{2,1,0:T(8,128)}, f32[1,768,768]{2,1,0:T(8,128)}), (f32[1,768,768]{2,1,0:T(8,128)}, f32[1,768,768]{2,1,0:T(8,128)})) %all-reduce.4.cloned.1.call-update) | async-done | bytes 4718608 | tf_op jit(solution)/shard_map/psum | solution.py:14
  472.4 2.1 fusion.8
  474.5 14.5 %all-gather.5.cloned.1.call-done = bf16[6,768,768]{2,1,0:T(8,128)(2,1)} async-done(((bf16[6,96,768]{2,1,0:T(8,128)(2,1)}), bf16[6,768,768]{2,1,0:T(8,128)(2,1)}) %all-gather.5.cloned.1.call-update) | async-done | bytes 7077904 | tf_op jit(solution)/shard_map/all_gather | solution.py:61
  489.0 23.5 %all-gather.3.cloned.1.call-done = f32[8,96,768]{2,1,0:T(8,128)} async-done(((f32[2,96,768]{2,1,0:T(8,128)}), f32[8,96,768]{2,1,0:T(8,128)}) %all-gather.3.cloned.1.call-update) | async-done | bytes 2359312 | tf_op jit(solution)/shard_map/all_gather | solution.py:54
  512.5 6.7 %fusion.42 = f32[6,96,768]{2,1,0:T(8,128)S(1)} fusion(f32[8,96,768]{2,1,0:T(8,128)} %all-gather.3.cloned.1.call-done, bf16[6,768,768]{2,1,0:T(8,128)(2,1)} %all-gather.5.cloned.1.call-done), kind=kOutput, calls=%fused_computation.67 | convolution fusion | flops 4076863488 | bytes 11206656 | tf_op jit(solution)/shard_map/wrn,wnd->wrd/dot_general | solution.py:63
  (39 shorter events, 9.1 us)
Async XLA Ops:
  7.4 1.0 copy-start
  7.4 7.6 %copy-start.7 = (bf16[5,256,768]{2,1,0:T(8,128)(2,1)S(1)}, bf16[5,256,768]{2,1,0:T(8,128)(2,1)}, u32[]{:S(2)}) copy-start(bf16[5,256,768]{2,1,0:T(8,128)(2,1)} %param.7) | copy-start | bytes 5898244
  7.4 96.8 %reduce-scatter.2.cloned.1.call-start = ((), (), s32[]{:S(2)}) async-start(), calls=%async_computation.1 | async-start | bytes 11796480 | tf_op jit(solution)/shard_map/reduce_scatter | solution.py:37
  12.3 8.9 %copy-start.6 = (bf16[32,768]{1,0:T(8,128)(2,1)S(1)}, bf16[32,768]{1,0:T(8,128)(2,1)}, u32[]{:S(2)}) copy-start(bf16[32,768]{1,0:T(8,128)(2,1)} %param.9) | copy-start | bytes 147460
  22.9 449.5 %all-reduce.4.cloned.1.call-start = ((), (), s32[]{:S(2)}) async-start(), calls=%async_computation.4 | async-start | bytes 9437184 | tf_op jit(solution)/shard_map/psum | solution.py:14
  291.9 3.8 copy-start.2
  298.7 15.6 %copy-start.4 = (f32[768,768]{1,0:T(8,128)S(1)}, f32[768,768]{1,0:T(8,128)}, u32[]{:S(2)}) copy-start(f32[768,768]{1,0:T(8,128)} %fusion.26) | copy-start | bytes 7077892
  298.7 28.4 %slice-start = ((s8[4718592]{0:T(1024)(128)(4,1)}), s8[4194304]{0:T(1024)(128)(4,1)S(1)}, s32[]{:S(2)}) async-start(s8[4718592]{0:T(1024)(128)(4,1)} %bitcast.79), calls=%async_computation.5 | async-start | bytes 8388608
  314.3 12.9 %slice-start.1 = ((s8[4718592]{0:T(1024)(128)(4,1)}), s8[524288]{0:T(1024)(128)(4,1)S(1)}, s32[]{:S(2)}) async-start(s8[4718592]{0:T(1024)(128)(4,1)} %bitcast.79), calls=%async_computation.6 | async-start | bytes 1048576
  376.8 3.6 copy-start.3
  380.5 108.5 %all-gather.5.cloned.1.call-start = ((), (), s32[]{:S(2)}) async-start(), calls=%async_computation.3 | async-start | bytes 7962624 | tf_op jit(solution)/shard_map/all_gather | solution.py:61
  381.1 131.4 %all-gather.3.cloned.1.call-start = ((), (), s32[]{:S(2)}) async-start(), calls=%async_computation.2 | async-start | bytes 2949120 | tf_op jit(solution)/shard_map/all_gather | solution.py:54
  474.5 46.7 %copy-start.5 = (f32[6,96,192]{2,1,0:T(8,128)S(1)}, f32[6,96,192]{2,1,0:T(8,128)}, u32[]{:S(2)}) copy-start(f32[6,96,192]{2,1,0:T(8,128)} %param.11) | copy-start | bytes 1327108
  512.5 9.5 %copy-start.1 = (bf16[256,768]{1,0:T(8,128)(2,1)S(1)}, bf16[256,768]{1,0:T(8,128)(2,1)}, u32[]{:S(2)}) copy-start(bf16[256,768]{1,0:T(8,128)(2,1)} %param.6) | copy-start | bytes 1179652
Sparse Core Ops, SparseCore 0:
  23.0 81.1 reduce-scatter.1
  380.6 91.7 all-reduce.3
Sparse Core Ops, SparseCore 1:
  383.2 105.8 all-gather.4
  490.4 22.1 all-gather.2
where the time goes:
time: 534 us; the launch traced here: 530 us
  waiting for transfers between devices  207 us (39%)
  blocking collectives  188 us (35%)
  matrix products  101 us (19%)
  between operations  15.3 us (3%)
  other arithmetic  14.3 us (3%)
    psum x1, blocking collectives, on_device(): factor_full = lax.psum(summed, 'shard')  188 us
    psum x1, waiting for transfers between devices, broadcast(): return lax.psum(jnp.where(mine, array, jnp.zeros_like(array)), axis)  89.3 us
    reduce_scatter x1, waiting for transfers between devices, on_device(): lax.psum_scatter(stacked, 'group', scatter_dimension=0, tiled=True)  79.3 us
    dot_general x3, matrix products, on_device(): product = jnp.einsum('kij,kjl->kil', matrix, approx, precision=PRECISE)  39.9 us
    dot_general x3, matrix products, on_device(): jnp.einsum('kij,kjl->kil', approx, product, precision=PRECISE)  38.1 us
    all_gather x1, waiting for transfers between devices, on_device(): all_rows = lax.all_gather(own_rows, 'group', axis=0, tiled=True)  23.5 us
    all_gather x1, waiting for transfers between devices, on_device(): gathered = lax.all_gather(weight_grads, 'shard', axis=1, tiled=True)  14.5 us
    dot_general x8, matrix products, outer_sum(): lax.dot_general(matrix_rows, matrix_rows, (((0,), (0,)), ((), ())), prefe...  14.5 us
  transfers between devices with their start and end apart: 4, of which 4 were waited for; matrix products, arithmetic and copies ran while one was open for 1% of the time, Pallas kernels for 0%

commit v1 on v0

--- a/solution.py
+++ b/solution.py
@@ -7,6 +7,12 @@
 PRECISE = lax.Precision.HIGHEST
 DAMPING = 0.1
 MOMENTUM = 0.9
+
+
+def joined_along(blocks, dim):
+    dims = list(blocks.shape[1:])
+    dims[dim] *= blocks.shape[0]
+    return jnp.moveaxis(blocks, 0, dim).reshape(dims)
 
 
 def broadcast(array, axis, root):
@@ -58,7 +64,19 @@
     input_cols = lax.dynamic_slice_in_dim(input_inv, group_pos * col_block, col_block, 2)
     out_inverse = all_rows[2:8]
     initial = jnp.zeros(out_inverse.shape, jnp.float32)
-    gathered = lax.all_gather(weight_grads, "shard", axis=1, tiled=True)
+    count = lax.axis_size("shard")
+    pairs = [(i, (i + 1) % count) for i in range(count)]
+    back = [(b, a) for a, b in pairs]
+    lower, upper = ([], [])
+    for step in range(count - 1):
+        if step % 2 == 0:
+            lower.append(lax.ppermute(lower[-1] if lower else weight_grads, "shard", pairs))
+        else:
+            upper.append(lax.ppermute(upper[-1] if upper else weight_grads, "shard", back))
+    pieces = jnp.stack([*lower[::-1], weight_grads, *upper])
+    shift = lax.axis_index("shard") - len(lower)
+    pieces = pieces[(jnp.arange(count) - shift) % count]
+    gathered = joined_along(pieces, 1)
     columns = lax.slice_in_dim(out_inverse, 0, gathered.shape[1], axis=2)
     left_side = initial + jnp.einsum(
         "wrn,wnd->wrd", columns, gathered.astype(jnp.float32), precision=PRECISE

time: 534 us -> 571 us (1.069)
  local copies, waits for them, and re-layouts: 4.07 us -> 31.1 us
  starting transfers between devices: 0.13 us -> 14.3 us
    ppermute x0 -> x7, waiting for transfers between devices: none -> 125 us  [the longest x4 125 us: on_device(): lax.ppermute(lower[-1] if lower else weight_grads, 'shard', pairs)]
    psum x1, waiting for transfers between devices: 89.3 us -> 0.01 us  [broadcast(): return lax.psum(jnp.where(mine, array, jnp.zeros_like(array)), axis)]
    all_gather x1, waiting for transfers between devices: 23.5 us -> 0.02 us  [on_device(): all_rows = lax.all_gather(own_rows, 'group', axis=0, tiled=True)]
    all_gather x1 -> x0, waiting for transfers between devices: 14.5 us -> none  [on_device(): gathered = lax.all_gather(weight_grads, 'shard', axis=1, tiled=True)]
    ppermute x0 -> x7, starting transfers between devices: none -> 14.2 us  [the longest x3 9.11 us: on_device(): lax.ppermute(upper[-1] if upper else weight_grads, 'shard', back)]
    unnamed x20 -> x29, local copies, waits for them, and re-layouts: 2.14 us -> 14.7 us
    gather x0 -> x1, local copies, waits for them, and re-layouts: none -> 6.94 us  [on_device(): pieces = pieces[(jnp.arange(count) - shift) % count]]
    transpose x0 -> x1, local copies, waits for them, and re-layouts: none -> 6.48 us  [joined_along(): return jnp.moveaxis(blocks, 0, dim).reshape(dims)]
  transfers between devices with their start and end apart: 4 -> 10, of which waited for: 4 -> 6; matrix products, arithmetic and copies ran while one was open for 1% -> 6% of each run, Pallas kernels for 0% -> 0%
where the time goes in v1:
time: 571 us; the launch traced here: 567 us
  waiting for transfers between devices  204 us (36%)
  blocking collectives  188 us (33%)
  matrix products  101 us (18%)
  local copies, waits for them, and re-layouts  31.1 us (5%)
  other arithmetic  14.4 us (3%)
  starting transfers between devices  14.3 us (3%)
  between operations  13.6 us (2%)
    psum x1, blocking collectives, on_device(): factor_full = lax.psum(summed, 'shard')  188 us
    ppermute x4, waiting for transfers between devices, on_device(): lax.ppermute(lower[-1] if lower else weight_grads, 'shard', pairs)  125 us
    reduce_scatter x1, waiting for transfers between devices, on_device(): lax.psum_scatter(stacked, 'group', scatter_dimension=0, tiled=True)  79.3 us
    dot_general x3, matrix products, on_device(): product = jnp.einsum('kij,kjl->kil', matrix, approx, precision=PRECISE)  39.9 us
    dot_general x3, matrix products, on_device(): jnp.einsum('kij,kjl->kil', approx, product, precision=PRECISE)  38.1 us
    unnamed x29, local copies, waits for them, and re-layouts  14.7 us
    dot_general x8, matrix products, outer_sum(): lax.dot_general(matrix_rows, matrix_rows, (((0,), (0,)), ((), ())), prefe...  14.4 us
  transfers between devices with their start and end apart: 10, of which 6 were waited for; matrix products, arithmetic and copies ran while one was open for 6% of the time, Pallas kernels for 0%

profile of v1, /device:TPU:0, one launch (start us, length us, event | category | flops | bytes accessed | tf_op | source)
XLA Modules:
  0.0 566.6 jit_solution(3289695033950375229)
XLA Ops:
  9.1 2.4 fusion.10
  11.5 2.7 fusion.16
  24.0 79.3 %reduce-scatter.2.cloned.1.call-done = bf16[2,768,768]{2,1,0:T(8,128)(2,1)} async-done(((bf16[8,768,768]{2,1,0:T(8,128)(2,1)}), bf16[2,768,768]{2,1,0:T(8,128)(2,1)}) %reduce-scatter.2.cloned.1.call-update) | async-done | bytes 2359312 | tf_op jit(solution)/shard_map/reduce_scatter | solution.py:43
  103.3 187.8 %all-reduce.5 = f32[2,768,768]{2,1,0:T(8,128)} all-reduce(bf16[2,768,768]{2,1,0:T(8,128)(2,1)} %reduce-scatter.2.cloned.1.call-done), channel_id=1, replica_groups=mesh['group'=4,'shard'=8] {'shard'}, use_global_device_ids=true, to_apply=%region_1.2 | all-reduce | flops 1179648 | bytes 7077888 | tf_op jit(solution)/shard_map/psum | solution.py:49
  291.0 3.7 select_reduce_fusion
  294.8 3.0 abs_reduce_fusion
  297.9 15.5 %fusion.2 = f32[2,768,768]{2,1,0:T(8,128)S(1)} fusion(f32[2,768,768]{2,1,0:T(8,128)} %get-tuple-element.8, f32[2]{0:T(128)S(1)} %reduce_max.9, f32[768,768]{1,0:T(8,128)} %fusion.26), kind=kOutput, calls=%fused_computation.11 | convolution fusion | flops 10872815616 | bytes 11796488 | tf_op jit(solution)/shard_map/kij,kjl->kil/dot_general | solution.py:57
  313.4 12.8 %multiply_subtract_fusion.2 = f32[2,768,768]{2,1,0:T(8,128)S(1)} fusion(f32[2]{0:T(128)S(1)} %reduce_max.9, f32[768,768]{1,0:T(8,128)S(1)} %copy-done.4, f32[2,768,768]{2,1,0:T(8,128)S(1)} %fusion.2), kind=kOutput, calls=%fused_computation.5 | convolution fusion | flops 10876354560 | bytes 11796488 | tf_op jit(solution)/shard_map/kij,kjl->kil/dot_general | solution.py:58
  326.3 12.1 %fusion.42 = f32[2,768,768]{2,1,0:T(8,128)S(1)} fusion(f32[2,768,768]{2,1,0:T(8,128)S(1)} %bitcast.100, f32[2,768,768]{2,1,0:T(8,128)S(1)} %multiply_subtract_fusion.2), kind=kOutput, calls=%fused_computation.81 | convolution fusion | flops 10871635968 | bytes 14155776 | tf_op jit(solution)/shard_map/kij,kjl->kil/dot_general | solution.py:57
  338.4 12.7 %multiply_subtract_fusion.1 = f32[2,768,768]{2,1,0:T(8,128)S(1)} fusion(f32[2,768,768]{2,1,0:T(8,128)S(1)} %multiply_subtract_fusion.2, f32[2,768,768]{2,1,0:T(8,128)S(1)} %fusion.42), kind=kOutput, calls=%fused_computation.4 | convolution fusion | flops 10873995264 | bytes 14155776 | tf_op jit(solution)/shard_map/kij,kjl->kil/dot_general | solution.py:58
  351.1 12.3 %fusion.43 = f32[2,768,768]{2,1,0:T(8,128)S(1)} fusion(f32[2,768,768]{2,1,0:T(8,128)S(1)} %bitcast.100, f32[2,768,768]{2,1,0:T(8,128)S(1)} %multiply_subtract_fusion.1), kind=kOutput, calls=%fused_computation.82 | convolution fusion | flops 10871635968 | bytes 14155776 | tf_op jit(solution)/shard_map/kij,kjl->kil/dot_general | solution.py:57
  363.4 12.5 %multiply_subtract_fusion = f32[2,768,768]{2,1,0:T(8,128)S(1)} fusion(f32[2,768,768]{2,1,0:T(8,128)S(1)} %multiply_subtract_fusion.1, f32[2,768,768]{2,1,0:T(8,128)S(1)} %fusion.43), kind=kOutput, calls=%fused_computation.3 | convolution fusion | flops 10873995264 | bytes 14155776 | tf_op jit(solution)/shard_map/kij,kjl->kil/dot_general | solution.py:58
  375.9 2.7 slice_select_fusion
  380.8 23.7 %collective-permute-done = bf16[6,96,768]{2,1,0:T(8,128)(2,1)S(1)} collective-permute-done((bf16[6,96,768]{2,1,0:T(8,128)(2,1)S(1)}, bf16[6,96,768]{2,1,0:T(8,128)(2,1)S(1)}, u32[]{:S(2)}, u32[]{:S(2)}) %collective-permute-start) | collective-permute-done | bytes 884768 | tf_op jit(solution)/shard_map/ppermute | solution.py:73
  404.5 4.7 collective-permute-start.4
  409.3 31.7 %collective-permute-done.1 = bf16[6,96,768]{2,1,0:T(8,128)(2,1)} collective-permute-done((bf16[6,96,768]{2,1,0:T(8,128)(2,1)S(1)}, bf16[6,96,768]{2,1,0:T(8,128)(2,1)}, u32[]{:S(2)}, u32[]{:S(2)}) %collective-permute-start.1) | collective-permute-done | bytes 884768 | tf_op jit(solution)/shard_map/ppermute | solution.py:73
  440.9 2.6 collective-permute-start.2
  447.7 34.2 %collective-permute-done.2 = bf16[6,96,768]{2,1,0:T(8,128)(2,1)} collective-permute-done((bf16[6,96,768]{2,1,0:T(8,128)(2,1)}, bf16[6,96,768]{2,1,0:T(8,128)(2,1)}, u32[]{:S(2)}, u32[]{:S(2)}) %collective-permute-start.2) | collective-permute-done | bytes 884768 | tf_op jit(solution)/shard_map/ppermute | solution.py:73
  481.9 2.5 collective-permute-start.3
  484.5 2.2 collective-permute-start.6
  486.7 35.2 %collective-permute-done.3 = bf16[6,96,768]{2,1,0:T(8,128)(2,1)} collective-permute-done((bf16[6,96,768]{2,1,0:T(8,128)(2,1)}, bf16[6,96,768]{2,1,0:T(8,128)(2,1)}, u32[]{:S(2)}, u32[]{:S(2)}) %collective-permute-start.3) | collective-permute-done | bytes 884768 | tf_op jit(solution)/shard_map/ppermute | solution.py:73
  534.4 6.9 %gather_fusion = bf16[8,6,96,768]{3,2,1,0:T(8,128)(2,1)} fusion(bf16[8,6,96,768]{3,2,1,0:T(8,128)(2,1)} %bitcast_dynamic-update-slice_fusion, s32[1024]{0:T(1024)S(1)} %pad_clamp_fusion), kind=kCustom, calls=%fused_computation | custom fusion | bytes 14155808 | tf_op jit(solution)/shard_map/gather | solution.py:78
  541.4 6.5 %copy.13 = bf16[6,8,96,768]{3,2,1,0:T(8,128)(2,1)} copy(bf16[6,8,96,768]{3,2,0,1:T(8,128)(2,1)} %bitcast.101) | data formatting | bytes 14155776 | tf_op jit(solution)/shard_map/transpose | solution.py:15
  550.0 7.0 %fusion.44 = f32[6,96,768]{2,1,0:T(8,128)S(1)} fusion(f32[8,96,768]{2,1,0:T(8,128)} %all-gather.2.cloned.1.call-done, bf16[6,768,768]{2,1,0:T(8,128)(2,1)} %bitcast.102), kind=kOutput, calls=%fused_computation.83 | convolution fusion | flops 4076863488 | bytes 11206656 | tf_op jit(solution)/shard_map/wrn,wnd->wrd/dot_general | solution.py:81
  (64 shorter events, 36.4 us)
Async XLA Ops:
  6.5 1.0 copy-start
  6.5 7.6 %copy-start.8 = (bf16[5,256,768]{2,1,0:T(8,128)(2,1)S(1)}, bf16[5,256,768]{2,1,0:T(8,128)(2,1)}, u32[]{:S(2)}) copy-start(bf16[5,256,768]{2,1,0:T(8,128)(2,1)} %param.7) | copy-start | bytes 5898244
  6.5 96.7 %reduce-scatter.2.cloned.1.call-start = ((), (), s32[]{:S(2)}) async-start(), calls=%async_computation.1 | async-start | bytes 11796480 | tf_op jit(solution)/shard_map/reduce_scatter | solution.py:43
  11.5 8.9 %copy-start.7 = (bf16[32,768]{1,0:T(8,128)(2,1)S(1)}, bf16[32,768]{1,0:T(8,128)(2,1)}, u32[]{:S(2)}) copy-start(bf16[32,768]{1,0:T(8,128)(2,1)} %param.9) | copy-start | bytes 147460
  22.0 525.9 %all-reduce.4.cloned.1.call-start = ((), (), s32[]{:S(2)}) async-start(), calls=%async_computation.3 | async-start | bytes 9437184 | tf_op jit(solution)/shard_map/psum | solution.py:20
  291.0 3.8 copy-start.2
  297.9 15.5 %copy-start.4 = (f32[768,768]{1,0:T(8,128)S(1)}, f32[768,768]{1,0:T(8,128)}, u32[]{:S(2)}) copy-start(f32[768,768]{1,0:T(8,128)} %fusion.26) | copy-start | bytes 7077892
  297.9 28.4 %slice-start = ((s8[4718592]{0:T(1024)(128)(4,1)}), s8[4194304]{0:T(1024)(128)(4,1)S(1)}, s32[]{:S(2)}) async-start(s8[4718592]{0:T(1024)(128)(4,1)} %bitcast.99), calls=%async_computation.4 | async-start | bytes 8388608
  313.4 12.9 %slice-start.1 = ((s8[4718592]{0:T(1024)(128)(4,1)}), s8[524288]{0:T(1024)(128)(4,1)S(1)}, s32[]{:S(2)}) async-start(s8[4718592]{0:T(1024)(128)(4,1)} %bitcast.99), calls=%async_computation.5 | async-start | bytes 1048576
  375.9 3.7 copy-start.3
  379.6 1.2 copy-start.5
  379.6 170.3 %all-gather.2.cloned.1.call-start = ((), (), s32[]{:S(2)}) async-start(), calls=%async_computation.2 | async-start | bytes 2949120 | tf_op jit(solution)/shard_map/all_gather | solution.py:60
  380.8 23.7 %collective-permute-start = (bf16[6,96,768]{2,1,0:T(8,128)(2,1)S(1)}, bf16[6,96,768]{2,1,0:T(8,128)(2,1)S(1)}, u32[]{:S(2)}, u32[]{:S(2)}) collective-permute-start(bf16[6,96,768]{2,1,0:T(8,128)(2,1)S(1)} %copy-done.5), channel_id=1, source_target_pairs={{0,1},{1,2},{2,3},{3,4},{4,5},{5,6},{6,7},{7,0},{8,9},{9,10},{10,1... | collective-permute-start | bytes 2654216 | tf_op jit(solution)/shard_map/ppermute | solution.py:73
  404.5 36.4 %collective-permute-start.1 = (bf16[6,96,768]{2,1,0:T(8,128)(2,1)S(1)}, bf16[6,96,768]{2,1,0:T(8,128)(2,1)}, u32[]{:S(2)}, u32[]{:S(2)}) collective-permute-start(bf16[6,96,768]{2,1,0:T(8,128)(2,1)S(1)} %collective-permute-done), channel_id=1, source_target_pairs={{0,1},{1,2},{2,3},{3,4},{4,5},{5,6},{6,7},{7,0},{8,9},{9,10},{10,1... | collective-permute-start | bytes 2654216 | tf_op jit(solution)/shard_map/ppermute | solution.py:73
  404.5 40.9 %collective-permute-start.4 = (bf16[6,96,768]{2,1,0:T(8,128)(2,1)S(1)}, bf16[6,96,768]{2,1,0:T(8,128)(2,1)S(1)}, u32[]{:S(2)}, u32[]{:S(2)}) collective-permute-start(bf16[6,96,768]{2,1,0:T(8,128)(2,1)S(1)} %copy-done.5), channel_id=1, source_target_pairs={{1,0},{2,1},{3,2},{4,3},{5,4},{6,5},{7,6},{0,7},{9,8},{10,9},{11,1... | collective-permute-start | bytes 2654216 | tf_op jit(solution)/shard_map/ppermute | solution.py:75
  440.9 41.0 %collective-permute-start.2 = (bf16[6,96,768]{2,1,0:T(8,128)(2,1)}, bf16[6,96,768]{2,1,0:T(8,128)(2,1)}, u32[]{:S(2)}, u32[]{:S(2)}) collective-permute-start(bf16[6,96,768]{2,1,0:T(8,128)(2,1)} %collective-permute-done.1), channel_id=1, source_target_pairs={{0,1},{1,2},{2,3},{3,4},{4,5},{5,6},{6,7},{7,0},{8,9},{9,10},{10,1... | collective-permute-start | bytes 2654216 | tf_op jit(solution)/shard_map/ppermute | solution.py:73
  445.5 39.0 %collective-permute-start.5 = (bf16[6,96,768]{2,1,0:T(8,128)(2,1)S(1)}, bf16[6,96,768]{2,1,0:T(8,128)(2,1)}, u32[]{:S(2)}, u32[]{:S(2)}) collective-permute-start(bf16[6,96,768]{2,1,0:T(8,128)(2,1)S(1)} %collective-permute-done.4), channel_id=1, source_target_pairs={{1,0},{2,1},{3,2},{4,3},{5,4},{6,5},{7,6},{0,7},{9,8},{10,9},{11,1... | collective-permute-start | bytes 2654216 | tf_op jit(solution)/shard_map/ppermute | solution.py:75
  481.9 40.0 %collective-permute-start.3 = (bf16[6,96,768]{2,1,0:T(8,128)(2,1)}, bf16[6,96,768]{2,1,0:T(8,128)(2,1)}, u32[]{:S(2)}, u32[]{:S(2)}) collective-permute-start(bf16[6,96,768]{2,1,0:T(8,128)(2,1)} %collective-permute-done.2), channel_id=1, source_target_pairs={{0,1},{1,2},{2,3},{3,4},{4,5},{5,6},{6,7},{7,0},{8,9},{9,10},{10,1... | collective-permute-start | bytes 2654216 | tf_op jit(solution)/shard_map/ppermute | solution.py:73
  484.5 49.0 %collective-permute-start.6 = (bf16[6,96,768]{2,1,0:T(8,128)(2,1)}, bf16[6,96,768]{2,1,0:T(8,128)(2,1)S(1)}, u32[]{:S(2)}, u32[]{:S(2)}) collective-permute-start(bf16[6,96,768]{2,1,0:T(8,128)(2,1)} %collective-permute-done.5), channel_id=1, source_target_pairs={{1,0},{2,1},{3,2},{4,3},{5,4},{6,5},{7,6},{0,7},{9,8},{10,9},{11,1... | collective-permute-start | bytes 2654216 | tf_op jit(solution)/shard_map/ppermute | solution.py:75
  550.0 8.9 %copy-start.6 = (f32[6,96,192]{2,1,0:T(8,128)S(1)}, f32[6,96,192]{2,1,0:T(8,128)}, u32[]{:S(2)}) copy-start(f32[6,96,192]{2,1,0:T(8,128)} %param.11) | copy-start | bytes 1327108
  550.0 9.8 %copy-start.1 = (bf16[256,768]{1,0:T(8,128)(2,1)S(1)}, bf16[256,768]{1,0:T(8,128)(2,1)}, u32[]{:S(2)}) copy-start(bf16[256,768]{1,0:T(8,128)(2,1)} %param.6) | copy-start | bytes 1179652
Sparse Core Ops, SparseCore 0:
  22.1 81.1 reduce-scatter.1
  379.8 91.6 all-reduce.3
  473.1 24.2 all-gather.1
